TPU v7x, 32 devices: a whole 2x2x4 slice. The times are simulated.
32 devices in a mesh: pat: 4 (over z), vox: 8 (over y, x, core).
Axes of the slice: x: 2, y: 2, z: 4, core: 2. Of those that a mesh axis runs over, the one named last changes fastest.
Arguments:
- conductivity: float32 [16, 128, 128], P('vox'), may hold values from 0.3 to 1.5
- warm_forward: float32 [16, 32, 128, 128], P('vox', 'pat'), may hold values from -3 to 3
- warm_adjoint: float32 [16, 32, 128, 128], P('vox', 'pat'), may hold values from -3 to 3
- electrodes: int32 [128], replicated, may hold values from 0 to 262143
- patterns: int32 [32, 4], P('pat'), may hold values from 0 to 127, all different within a row
- observed: float32 [32], P('pat'), may hold values from -16 to 16
Outputs:
- gradient: float32 [16, 128, 128], P('vox')
- predicted: float32 [32], P('pat')
All inputs are finite; a program needn't handle non-finite values.
Results may differ from a plain program's by a relative error of at most 0.0003.
Values sent between devices are 32-bit elements; how exact they have to be, the bound alone decides.
No kernel may reach another device: no remote copies, remote signals or barrier semaphores. Data moves between devices by JAX's collectives and lax.ppermute only.
A program may use at most 64 MiB of HBM per device.

v0:
```python
import math
import jax
import jax.numpy as jnp
from jax import lax
from jax.sharding import PartitionSpec as P

ITERS = 2
leakage = 0.05


def extended(block, sides, width):
    for axis, dim in sides:
        count = lax.axis_size(axis)
        forward = [(i, i + 1) for i in range(count - 1)]
        backward = [(target, source) for source, target in forward]
        low = lax.ppermute(
            lax.slice_in_dim(block, block.shape[dim] - width, None, axis=dim), axis, forward
        )
        high = lax.ppermute(lax.slice_in_dim(block, 0, width, axis=dim), axis, backward)
        block = jnp.concatenate([low, block, high], axis=dim)
    return block


def both_sides(values, along_axis):
    lower_pad = [(0, 0)] * values.ndim
    upper_pad = [(0, 0)] * values.ndim
    lower_pad[along_axis] = (1, 0)
    upper_pad[along_axis] = (0, 1)
    return jnp.pad(values, lower_pad) + jnp.pad(values, upper_pad)


def spread(values, along_axis):
    lower_pad = [(0, 0)] * values.ndim
    upper_pad = [(0, 0)] * values.ndim
    lower_pad[along_axis] = (1, 0)
    upper_pad[along_axis] = (0, 1)
    return jnp.pad(values, lower_pad) - jnp.pad(values, upper_pad)


def operate(values, coeffs):
    depth_faces, row_faces, column_faces = coeffs
    padded = extended(values, (("vox", 0),), 1)
    flux_depth = depth_faces[:, None] * (padded[1:] - padded[:-1])
    result = leakage * values + (flux_depth[:-1] - flux_depth[1:])
    result = result + spread(row_faces[:, None] * (values[:, :, 1:] - values[:, :, :-1]), 2)
    result = result + spread(
        column_faces[:, None] * (values[:, :, :, 1:] - values[:, :, :, :-1]), 3
    )
    return result


def inner(left_factor, right_factor):
    return jnp.sum(left_factor * right_factor, axis=(0, 2, 3))


def widen(vector):
    return vector[None, :, None, None]


def pattern_sum(local_terms):
    return lax.psum(local_terms, "vox")


def solve_pattern(right_side, initial, coeffs, diagonal):
    solution = initial
    residue = right_side - operate(solution, coeffs)
    precond = residue / diagonal
    direction = precond
    current = pattern_sum(inner(residue, precond))
    for iteration in range(ITERS):
        applied = operate(direction, coeffs)
        step_size = current / pattern_sum(inner(direction, applied))
        solution = solution + widen(step_size) * direction
        residue = residue - widen(step_size) * applied
        if iteration + 1 < ITERS:
            precond = residue / diagonal
            following = pattern_sum(inner(residue, precond))
            direction = precond + widen(following / current) * direction
            current = following
    return solution


def per_device(conductivity, warm_forward, warm_adjoint, electrodes, patterns, observed):
    plane_count, pattern_count, row_count, column_count = warm_forward.shape
    position = lax.axis_index("vox")
    layers = lax.axis_size("vox")
    strength = 2.0 * math.sqrt(layers * plane_count * row_count * column_count)
    data_weight = 0.1 * strength
    lower_open = (position > 0).astype(jnp.float32)
    upper_open = (position < layers - 1).astype(jnp.float32)
    padded_sigma = extended(conductivity, (("vox", 0),), 1)
    face_mask = jnp.concatenate(
        [lower_open[None], jnp.ones((plane_count - 1,), jnp.float32), upper_open[None]]
    )
    depth_faces = 0.5 * (padded_sigma[1:] + padded_sigma[:-1]) * face_mask[:, None, None]
    row_faces = 0.5 * (conductivity[:, 1:] + conductivity[:, :-1])
    column_faces = 0.5 * (conductivity[:, :, 1:] + conductivity[:, :, :-1])
    coeffs = (depth_faces, row_faces, column_faces)
    diagonal = (
        leakage
        + (depth_faces[:-1] + depth_faces[1:])
        + both_sides(row_faces, 1)
        + both_sides(column_faces, 2)
    )
    diagonal = diagonal[:, None]
    electrode_ids = jnp.arange(electrodes.shape[0], dtype=jnp.int32)
    picked = jnp.sum(
        jnp.where(
            patterns[:, :, None] == electrode_ids[None, None, :], electrodes[None, None, :], 0
        ),
        axis=2,
    )
    offset = position * (plane_count * row_count * column_count)
    local_cell = picked - offset
    grid_shape = (plane_count, 1, row_count, column_count)
    cell_index = (
        lax.broadcasted_iota(jnp.int32, grid_shape, 0) * row_count
        + lax.broadcasted_iota(jnp.int32, grid_shape, 2)
    ) * column_count + lax.broadcasted_iota(jnp.int32, grid_shape, 3)

    def marker(which_one):
        return (cell_index == local_cell[:, which_one][None, :, None, None]).astype(jnp.float32)

    forward = solve_pattern(strength * (marker(0) - marker(1)), warm_forward, coeffs, diagonal)
    probe_weights = marker(2) - marker(3)
    predicted = lax.psum(inner(probe_weights, forward), "vox")
    misfit = predicted - observed
    adjoint = solve_pattern(
        widen(data_weight * misfit) * probe_weights, warm_adjoint, coeffs, diagonal
    )
    stacked = jnp.concatenate([forward, adjoint], axis=1)
    padded_pair = extended(stacked, (("vox", 0),), 1)
    padded_forward = padded_pair[:, :pattern_count]
    padded_adjoint = padded_pair[:, pattern_count:]
    depth_products = jnp.sum(
        (padded_forward[1:] - padded_forward[:-1]) * (padded_adjoint[1:] - padded_adjoint[:-1]),
        axis=1,
    )
    depth_products = depth_products * face_mask[:, None, None]
    grad_depth = depth_products[:-1] + depth_products[1:]
    row_products = jnp.sum(
        (forward[:, :, 1:] - forward[:, :, :-1]) * (adjoint[:, :, 1:] - adjoint[:, :, :-1]), axis=1
    )
    column_products = jnp.sum(
        (forward[:, :, :, 1:] - forward[:, :, :, :-1])
        * (adjoint[:, :, :, 1:] - adjoint[:, :, :, :-1]),
        axis=1,
    )
    local_gradient = -0.5 * (
        grad_depth + both_sides(row_products, 1) + both_sides(column_products, 2)
    )
    gradient = lax.psum(local_gradient, "pat")
    return (gradient, predicted)


def solution(mesh):
    in_specs = (
        P("vox", None, None),
        P("vox", "pat", None, None),
        P("vox", "pat", None, None),
        P(),
        P("pat", None),
        P("pat"),
    )
    out_specs = (P("vox", None, None), P("pat"))
    return jax.shard_map(
        per_device, mesh=mesh, in_specs=in_specs, out_specs=out_specs, check_vma=False
    )
```

profile of v0, /device:TPU:0, one launch (start us, length us, event | category | flops | bytes accessed | tf_op | source)
XLA Modules:
  0.0 282.5 jit_solution(13601715273596078150)
XLA Ops:
  8.2 1.3 collective-permute-start
  9.5 3.0 %collective-permute-start.1 = (f32[1,128,128]{2,1,0:T(8,128)S(1)}, f32[1,128,128]{2,1,0:T(8,128)S(1)}, u32[]{:S(2)}, u32[]{:S(2)}) collective-permute-start(f32[1,128,128]{2,1,0:T(8,128)S(1)} %get-tuple-element.42), channel_id=1, source_target_pairs={{0,1},{1,2},{2,3},{3,4},{4,5},{5,6},{6,7},{8,9},{9,10},{10,11},{11... | collective-permute-start | bytes 196616 | tf_op jit(solution)/shard_map/ppermute | solution.py:16
  12.5 2.1 fusion.61
  14.6 1.4 collective-permute-start.2
  16.1 5.9 %collective-permute-start.3 = (f32[1,8,128,128]{3,2,1,0:T(8,128)S(1)}, f32[1,8,128,128]{3,2,1,0:T(8,128)}, u32[]{:S(2)}, u32[]{:S(2)}) collective-permute-start(f32[1,8,128,128]{3,2,1,0:T(8,128)S(1)} %get-tuple-element.32), channel_id=1, source_target_pairs={{0,1},{1,2},{2,3},{3,4},{4,5},{5,6},{6,7},{8,9},{9,10},{10,11},{11... | collective-permute-start | bytes 1572872 | tf_op jit(solution)/shard_map/ppermute | solution.py:16
  23.1 3.7 %collective-permute-start.9 = (f32[1,8,128,128]{3,2,1,0:T(8,128)}, f32[1,8,128,128]{3,2,1,0:T(8,128)}, u32[]{:S(2)}, u32[]{:S(2)}) collective-permute-start(f32[1,8,128,128]{3,2,1,0:T(8,128)} %get-tuple-element.34), channel_id=1, source_target_pairs={{0,1},{1,2},{2,3},{3,4},{4,5},{5,6},{6,7},{8,9},{9,10},{10,11},{11... | collective-permute-start | bytes 1572872 | tf_op jit(solution)/shard_map/ppermute | solution.py:16
  28.7 1.4 fusion.2
  31.0 1.4 collective-permute-start.4
  32.5 3.3 %collective-permute-start.5 = (f32[1,8,128,128]{3,2,1,0:T(8,128)S(1)}, f32[1,8,128,128]{3,2,1,0:T(8,128)S(1)}, u32[]{:S(2)}, u32[]{:S(2)}) collective-permute-start(f32[1,8,128,128]{3,2,1,0:T(8,128)S(1)} %get-tuple-element.30), channel_id=1, source_target_pairs={{0,1},{1,2},{2,3},{3,4},{4,5},{5,6},{6,7},{8,9},{9,10},{10,11},{11... | collective-permute-start | bytes 1572872 | tf_op jit(solution)/shard_map/ppermute | solution.py:16
  37.5 1.7 multiply_reduce_fusion.5
  39.2 27.2 %all-reduce.33 = (f32[8]{0:T(128)S(1)}, f32[8]{0:T(128)S(1)}) all-reduce(f32[8]{0:T(128)S(1)} %get-tuple-element.5, f32[8]{0:T(128)S(1)} %get-tuple-element.4), channel_id=1, replica_groups=mesh['pat'=4,'vox'=8] {'vox'}, use_global_device_ids=true, to_apply=%region_2.3 | all-reduce | flops 16 | bytes 128 | tf_op jit(solution)/shard_map/psum | solution.py:61
  66.5 1.6 multiply_reduce_fusion.4
  69.3 15.8 %psum.72 = f32[8]{0:T(128)S(1)} all-reduce(f32[8]{0:T(128)S(1)} %multiply_reduce_fusion.4), channel_id=1, replica_groups=mesh['pat'=4,'vox'=8] {'vox'}, use_global_device_ids=true, to_apply=%region_6.7 | all-reduce | flops 8 | bytes 64 | tf_op jit(solution)/shard_map/psum | solution.py:61
  85.2 1.8 multiply_add_fusion.3
  87.1 1.3 collective-permute-start.6
  88.4 3.2 %collective-permute-start.7 = (f32[1,8,128,128]{3,2,1,0:T(8,128)S(1)}, f32[1,8,128,128]{3,2,1,0:T(8,128)S(1)}, u32[]{:S(2)}, u32[]{:S(2)}) collective-permute-start(f32[1,8,128,128]{3,2,1,0:T(8,128)S(1)} %get-tuple-element.28), channel_id=1, source_target_pairs={{0,1},{1,2},{2,3},{3,4},{4,5},{5,6},{6,7},{8,9},{9,10},{10,11},{11... | collective-permute-start | bytes 1572872 | tf_op jit(solution)/shard_map/ppermute | solution.py:16
  91.6 1.6 fusion.29
  94.5 2.8 fusion.4
  98.0 20.6 %psum.73 = f32[8]{0:T(128)S(1)} all-reduce(f32[8]{0:T(128)S(1)} %fusion.35), channel_id=1, replica_groups=mesh['pat'=4,'vox'=8] {'vox'}, use_global_device_ids=true, to_apply=%region_8.9 | all-reduce | flops 8 | bytes 64 | tf_op jit(solution)/shard_map/psum | solution.py:61
  118.6 2.8 multiply_reduce_fusion.3
  121.4 12.4 %psum.74 = f32[8]{0:T(128)S(1)} all-reduce(f32[8]{0:T(128)S(1)} %get-tuple-element.15), channel_id=1, replica_groups=mesh['pat'=4,'vox'=8] {'vox'}, use_global_device_ids=true, to_apply=%region_10.11 | all-reduce | flops 8 | bytes 64 | tf_op jit(solution)/shard_map/psum | solution.py:126
  133.9 3.7 %broadcast_divide_fusion = (f32[2,8,128,128]{3,2,1,0:T(8,128)S(1)}, f32[2,8,128,128]{3,2,1,0:T(8,128)S(1)}) fusion(f32[2,128,128]{2,1,0:T(8,128)S(1)} %fusion.51, f32[2,8,128,127]{3,2,1,0:T(8,128)} %get-tuple-element.41, f32[2,8,127,128]{3,2,1,0:T(8,128)} %get-tuple-element.39, f32[3,8,128,128]{3,2,1,0:T(8,128)} %get-tuple-element.37, ...), kind=kLoop, calls=%fused_computation.94 | loop fusion | flops 3932160 | bytes 7585888 | tf_op jit(solution)/shard_map/div | solution.py:67
  137.7 1.3 collective-permute-start.10
  139.0 3.2 %collective-permute-start.11 = (f32[1,8,128,128]{3,2,1,0:T(8,128)S(1)}, f32[1,8,128,128]{3,2,1,0:T(8,128)S(1)}, u32[]{:S(2)}, u32[]{:S(2)}) collective-permute-start(f32[1,8,128,128]{3,2,1,0:T(8,128)S(1)} %get-tuple-element.26), channel_id=1, source_target_pairs={{0,1},{1,2},{2,3},{3,4},{4,5},{5,6},{6,7},{8,9},{9,10},{10,11},{11... | collective-permute-start | bytes 1572872 | tf_op jit(solution)/shard_map/ppermute | solution.py:16
  144.7 20.3 %all-reduce.32 = (f32[8]{0:T(128)S(1)}, f32[8]{0:T(128)S(1)}) all-reduce(f32[8]{0:T(128)S(1)} %get-tuple-element.3, f32[8]{0:T(128)S(1)} %get-tuple-element.2), channel_id=1, replica_groups=mesh['pat'=4,'vox'=8] {'vox'}, use_global_device_ids=true, to_apply=%region_12.13 | all-reduce | flops 16 | bytes 128 | tf_op jit(solution)/shard_map/psum | solution.py:61
  165.4 12.6 %psum.77 = f32[8]{0:T(128)S(1)} all-reduce(f32[8]{0:T(128)S(1)} %multiply_reduce_fusion), channel_id=1, replica_groups=mesh['pat'=4,'vox'=8] {'vox'}, use_global_device_ids=true, to_apply=%region_16.17 | all-reduce | flops 8 | bytes 64 | tf_op jit(solution)/shard_map/psum | solution.py:61
  178.0 1.5 multiply_add_fusion.1
  180.9 3.2 %collective-permute-start.13 = (f32[1,8,128,128]{3,2,1,0:T(8,128)S(1)}, f32[1,8,128,128]{3,2,1,0:T(8,128)S(1)}, u32[]{:S(2)}, u32[]{:S(2)}) collective-permute-start(f32[1,8,128,128]{3,2,1,0:T(8,128)S(1)} %get-tuple-element.24), channel_id=1, source_target_pairs={{0,1},{1,2},{2,3},{3,4},{4,5},{5,6},{6,7},{8,9},{9,10},{10,11},{11... | collective-permute-start | bytes 1572872 | tf_op jit(solution)/shard_map/ppermute | solution.py:16
  186.5 20.7 %psum.78 = f32[8]{0:T(128)S(1)} all-reduce(f32[8]{0:T(128)S(1)} %fusion.19), channel_id=1, replica_groups=mesh['pat'=4,'vox'=8] {'vox'}, use_global_device_ids=true, to_apply=%region_18.19 | all-reduce | flops 8 | bytes 64 | tf_op jit(solution)/shard_map/psum | solution.py:61
  210.0 3.1 %collective-permute-start.15 = (f32[1,16,128,128]{3,2,1,0:T(8,128)S(1)}, f32[1,16,128,128]{3,2,1,0:T(8,128)S(1)}, u32[]{:S(2)}, u32[]{:S(2)}) collective-permute-start(f32[1,16,128,128]{3,2,1,0:T(8,128)S(1)} %get-tuple-element.23), channel_id=1, source_target_pairs={{0,1},{1,2},{2,3},{3,4},{4,5},{5,6},{6,7},{8,9},{9,10},{10,11},{11... | collective-permute-start | bytes 3145736 | tf_op jit(solution)/shard_map/ppermute | solution.py:16
  217.7 56.4 %all-reduce.36.cloned.1.call-done = f32[2,128,128]{2,1,0:T(8,128)} async-done(((f32[2,128,128]{2,1,0:T(8,128)}), f32[2,128,128]{2,1,0:T(8,128)}) %all-reduce.36.cloned.1.call-update) | async-done | bytes 131088 | tf_op jit(solution)/shard_map/psum | solution.py:152
  274.0 1.6 copy.10
  (112 shorter events, 23.7 us)
Async XLA Ops:
  7.2 14.8 %copy-start = (f32[2,8,128,128]{3,2,1,0:T(8,128)S(1)}, f32[2,8,128,128]{3,2,1,0:T(8,128)}, u32[]{:S(2)}) copy-start(f32[2,8,128,128]{3,2,1,0:T(8,128)} %param.8) | copy-start | bytes 3145732
  7.2 266.9 %all-reduce.36.cloned.1.call-start = ((), (), s32[]{:S(2)}) async-start(), calls=%async_computation | async-start | bytes 262144 | tf_op jit(solution)/shard_map/psum | solution.py:152
  8.2 20.3 %collective-permute-start = (f32[1,128,128]{2,1,0:T(8,128)S(1)}, f32[1,128,128]{2,1,0:T(8,128)S(1)}, u32[]{:S(2)}, u32[]{:S(2)}) collective-permute-start(f32[1,128,128]{2,1,0:T(8,128)S(1)} %get-tuple-element.43), channel_id=1, source_target_pairs={{1,0},{2,1},{3,2},{4,3},{5,4},{6,5},{7,6},{9,8},{10,9},{11,10},{12... | collective-permute-start | bytes 196616 | tf_op jit(solution)/shard_map/ppermute | solution.py:19
  9.5 19.0 %collective-permute-start.1 = (f32[1,128,128]{2,1,0:T(8,128)S(1)}, f32[1,128,128]{2,1,0:T(8,128)S(1)}, u32[]{:S(2)}, u32[]{:S(2)}) collective-permute-start(f32[1,128,128]{2,1,0:T(8,128)S(1)} %get-tuple-element.42), channel_id=1, source_target_pairs={{0,1},{1,2},{2,3},{3,4},{4,5},{5,6},{6,7},{8,9},{9,10},{10,11},{11... | collective-permute-start | bytes 196616 | tf_op jit(solution)/shard_map/ppermute | solution.py:16
  14.6 12.1 %copy-start.15 = (f32[2,128,128]{2,1,0:T(8,128)S(1)}, f32[2,128,128]{2,1,0:T(8,128)}, u32[]{:S(2)}) copy-start(f32[2,128,128]{2,1,0:T(8,128)} %param.6) | copy-start | bytes 393220
  14.6 13.0 %copy-start.17 = (s32[8,4]{0,1:T(4,128)S(1)}, s32[8,4]{0,1:T(4,128)}, u32[]{:S(2)}) copy-start(s32[8,4]{0,1:T(4,128)} %param.10) | copy-start | bytes 388
  14.6 13.0 %copy-start.18 = (s32[128]{0:T(128)S(1)}, s32[128]{0:T(128)}, u32[]{:S(2)}) copy-start(s32[128]{0:T(128)} %param.9) | copy-start | bytes 1540
  14.6 13.3 %copy-start.1 = (f32[2,8,128,128]{3,2,1,0:T(8,128)S(1)}, f32[2,8,128,128]{3,2,1,0:T(8,128)}, u32[]{:S(2)}) copy-start(f32[2,8,128,128]{3,2,1,0:T(8,128)} %param.7) | copy-start | bytes 3145732
  14.6 14.1 %collective-permute-start.2 = (f32[1,8,128,128]{3,2,1,0:T(8,128)}, f32[1,8,128,128]{3,2,1,0:T(8,128)}, u32[]{:S(2)}, u32[]{:S(2)}) collective-permute-start(f32[1,8,128,128]{3,2,1,0:T(8,128)} %get-tuple-element.33), channel_id=1, source_target_pairs={{1,0},{2,1},{3,2},{4,3},{5,4},{6,5},{7,6},{9,8},{10,9},{11,10},{12... | collective-permute-start | bytes 1572872 | tf_op jit(solution)/shard_map/ppermute | solution.py:19
  16.1 12.7 %collective-permute-start.3 = (f32[1,8,128,128]{3,2,1,0:T(8,128)S(1)}, f32[1,8,128,128]{3,2,1,0:T(8,128)}, u32[]{:S(2)}, u32[]{:S(2)}) collective-permute-start(f32[1,8,128,128]{3,2,1,0:T(8,128)S(1)} %get-tuple-element.32), channel_id=1, source_target_pairs={{0,1},{1,2},{2,3},{3,4},{4,5},{5,6},{6,7},{8,9},{9,10},{10,11},{11... | collective-permute-start | bytes 1572872 | tf_op jit(solution)/shard_map/ppermute | solution.py:16
  23.1 71.4 %collective-permute-start.9 = (f32[1,8,128,128]{3,2,1,0:T(8,128)}, f32[1,8,128,128]{3,2,1,0:T(8,128)}, u32[]{:S(2)}, u32[]{:S(2)}) collective-permute-start(f32[1,8,128,128]{3,2,1,0:T(8,128)} %get-tuple-element.34), channel_id=1, source_target_pairs={{0,1},{1,2},{2,3},{3,4},{4,5},{5,6},{6,7},{8,9},{9,10},{10,11},{11... | collective-permute-start | bytes 1572872 | tf_op jit(solution)/shard_map/ppermute | solution.py:16
  30.9 35.5 %copy-start.3 = (f32[2,8,128,128]{3,2,1,0:T(8,128)}, f32[2,8,128,128]{3,2,1,0:T(8,128)S(1)}, u32[]{:S(2)}) copy-start(f32[2,8,128,128]{3,2,1,0:T(8,128)S(1)} %get-tuple-element.19) | copy-start | bytes 3145732
  31.0 4.9 %copy-start.11 = (f32[2,128,127]{2,1,0:T(8,128)S(1)}, f32[2,128,127]{2,1,0:T(8,128)}, u32[]{:S(2)}) copy-start(f32[2,128,127]{2,1,0:T(8,128)} %copy-done.10) | copy-start | bytes 390148
  31.0 5.3 %collective-permute-start.4 = (f32[1,8,128,128]{3,2,1,0:T(8,128)S(1)}, f32[1,8,128,128]{3,2,1,0:T(8,128)S(1)}, u32[]{:S(2)}, u32[]{:S(2)}) collective-permute-start(f32[1,8,128,128]{3,2,1,0:T(8,128)S(1)} %get-tuple-element.31), channel_id=1, source_target_pairs={{1,0},{2,1},{3,2},{4,3},{5,4},{6,5},{7,6},{9,8},{10,9},{11,10},{12... | collective-permute-start | bytes 1572872 | tf_op jit(solution)/shard_map/ppermute | solution.py:19
  32.5 3.7 %copy-start.6 = (f32[2,127,128]{2,1,0:T(8,128)S(1)}, f32[2,127,128]{2,1,0:T(8,128)}, u32[]{:S(2)}) copy-start(f32[2,127,128]{2,1,0:T(8,128)} %copy-done.5) | copy-start | bytes 390148
  32.5 4.8 %collective-permute-start.5 = (f32[1,8,128,128]{3,2,1,0:T(8,128)S(1)}, f32[1,8,128,128]{3,2,1,0:T(8,128)S(1)}, u32[]{:S(2)}, u32[]{:S(2)}) collective-permute-start(f32[1,8,128,128]{3,2,1,0:T(8,128)S(1)} %get-tuple-element.30), channel_id=1, source_target_pairs={{0,1},{1,2},{2,3},{3,4},{4,5},{5,6},{6,7},{8,9},{9,10},{10,11},{11... | collective-permute-start | bytes 1572872 | tf_op jit(solution)/shard_map/ppermute | solution.py:16
  68.0 26.5 %collective-permute-start.8 = (f32[1,8,128,128]{3,2,1,0:T(8,128)}, f32[1,8,128,128]{3,2,1,0:T(8,128)}, u32[]{:S(2)}, u32[]{:S(2)}) collective-permute-start(f32[1,8,128,128]{3,2,1,0:T(8,128)} %get-tuple-element.35), channel_id=1, source_target_pairs={{1,0},{2,1},{3,2},{4,3},{5,4},{6,5},{7,6},{9,8},{10,9},{11,10},{12... | collective-permute-start | bytes 1572872 | tf_op jit(solution)/shard_map/ppermute | solution.py:19
  87.0 4.6 %copy-start.12 = (f32[2,128,127]{2,1,0:T(8,128)S(1)}, f32[2,128,127]{2,1,0:T(8,128)}, u32[]{:S(2)}) copy-start(f32[2,128,127]{2,1,0:T(8,128)} %copy-done.10) | copy-start | bytes 390148
  87.1 7.4 %collective-permute-start.6 = (f32[1,8,128,128]{3,2,1,0:T(8,128)S(1)}, f32[1,8,128,128]{3,2,1,0:T(8,128)S(1)}, u32[]{:S(2)}, u32[]{:S(2)}) collective-permute-start(f32[1,8,128,128]{3,2,1,0:T(8,128)S(1)} %get-tuple-element.29), channel_id=1, source_target_pairs={{1,0},{2,1},{3,2},{4,3},{5,4},{6,5},{7,6},{9,8},{10,9},{11,10},{12... | collective-permute-start | bytes 1572872 | tf_op jit(solution)/shard_map/ppermute | solution.py:19
  88.4 4.8 %copy-start.7 = (f32[2,127,128]{2,1,0:T(8,128)S(1)}, f32[2,127,128]{2,1,0:T(8,128)}, u32[]{:S(2)}) copy-start(f32[2,127,128]{2,1,0:T(8,128)} %copy-done.5) | copy-start | bytes 390148
  88.4 6.1 %collective-permute-start.7 = (f32[1,8,128,128]{3,2,1,0:T(8,128)S(1)}, f32[1,8,128,128]{3,2,1,0:T(8,128)S(1)}, u32[]{:S(2)}, u32[]{:S(2)}) collective-permute-start(f32[1,8,128,128]{3,2,1,0:T(8,128)S(1)} %get-tuple-element.28), channel_id=1, source_target_pairs={{0,1},{1,2},{2,3},{3,4},{4,5},{5,6},{6,7},{8,9},{9,10},{10,11},{11... | collective-permute-start | bytes 1572872 | tf_op jit(solution)/shard_map/ppermute | solution.py:16
  118.6 15.3 %copy-start.19 = (f32[8]{0:T(128)S(1)}, f32[8]{0:T(128)}, u32[]{:S(2)}) copy-start(f32[8]{0:T(128)} %param.11) | copy-start | bytes 100
  133.9 3.8 %copy-start.20 = (f32[8]{0:T(128)}, f32[8]{0:T(128)S(1)}, u32[]{:S(2)}) copy-start(f32[8]{0:T(128)S(1)} %psum.74) | copy-start | bytes 100
  137.6 4.6 %copy-start.13 = (f32[2,128,127]{2,1,0:T(8,128)S(1)}, f32[2,128,127]{2,1,0:T(8,128)}, u32[]{:S(2)}) copy-start(f32[2,128,127]{2,1,0:T(8,128)} %copy-done.10) | copy-start | bytes 390148
  137.7 5.0 %collective-permute-start.10 = (f32[1,8,128,128]{3,2,1,0:T(8,128)S(1)}, f32[1,8,128,128]{3,2,1,0:T(8,128)S(1)}, u32[]{:S(2)}, u32[]{:S(2)}) collective-permute-start(f32[1,8,128,128]{3,2,1,0:T(8,128)S(1)} %get-tuple-element.27), channel_id=1, source_target_pairs={{1,0},{2,1},{3,2},{4,3},{5,4},{6,5},{7,6},{9,8},{10,9},{11,10},{12... | collective-permute-start | bytes 1572872 | tf_op jit(solution)/shard_map/ppermute | solution.py:19
  139.0 4.7 %collective-permute-start.11 = (f32[1,8,128,128]{3,2,1,0:T(8,128)S(1)}, f32[1,8,128,128]{3,2,1,0:T(8,128)S(1)}, u32[]{:S(2)}, u32[]{:S(2)}) collective-permute-start(f32[1,8,128,128]{3,2,1,0:T(8,128)S(1)} %get-tuple-element.26), channel_id=1, source_target_pairs={{0,1},{1,2},{2,3},{3,4},{4,5},{5,6},{6,7},{8,9},{9,10},{10,11},{11... | collective-permute-start | bytes 1572872 | tf_op jit(solution)/shard_map/ppermute | solution.py:16
  144.7 33.3 %copy-start.4 = (f32[2,8,128,128]{3,2,1,0:T(8,128)}, f32[2,8,128,128]{3,2,1,0:T(8,128)S(1)}, u32[]{:S(2)}) copy-start(f32[2,8,128,128]{3,2,1,0:T(8,128)S(1)} %get-tuple-element.12) | copy-start | bytes 3145732
  179.5 4.6 %copy-start.14 = (f32[2,128,127]{2,1,0:T(8,128)S(1)}, f32[2,128,127]{2,1,0:T(8,128)}, u32[]{:S(2)}) copy-start(f32[2,128,127]{2,1,0:T(8,128)} %copy-done.10) | copy-start | bytes 390148
  179.6 5.0 %collective-permute-start.12 = (f32[1,8,128,128]{3,2,1,0:T(8,128)S(1)}, f32[1,8,128,128]{3,2,1,0:T(8,128)S(1)}, u32[]{:S(2)}, u32[]{:S(2)}) collective-permute-start(f32[1,8,128,128]{3,2,1,0:T(8,128)S(1)} %get-tuple-element.25), channel_id=1, source_target_pairs={{1,0},{2,1},{3,2},{4,3},{5,4},{6,5},{7,6},{9,8},{10,9},{11,10},{12... | collective-permute-start | bytes 1572872 | tf_op jit(solution)/shard_map/ppermute | solution.py:19
  180.9 4.7 %collective-permute-start.13 = (f32[1,8,128,128]{3,2,1,0:T(8,128)S(1)}, f32[1,8,128,128]{3,2,1,0:T(8,128)S(1)}, u32[]{:S(2)}, u32[]{:S(2)}) collective-permute-start(f32[1,8,128,128]{3,2,1,0:T(8,128)S(1)} %get-tuple-element.24), channel_id=1, source_target_pairs={{0,1},{1,2},{2,3},{3,4},{4,5},{5,6},{6,7},{8,9},{9,10},{10,11},{11... | collective-permute-start | bytes 1572872 | tf_op jit(solution)/shard_map/ppermute | solution.py:16
  208.7 5.3 %collective-permute-start.14 = (f32[1,16,128,128]{3,2,1,0:T(8,128)S(1)}, f32[1,16,128,128]{3,2,1,0:T(8,128)S(1)}, u32[]{:S(2)}, u32[]{:S(2)}) collective-permute-start(f32[1,16,128,128]{3,2,1,0:T(8,128)S(1)} %get-tuple-element.22), channel_id=1, source_target_pairs={{1,0},{2,1},{3,2},{4,3},{5,4},{6,5},{7,6},{9,8},{10,9},{11,10},{12... | collective-permute-start | bytes 3145736 | tf_op jit(solution)/shard_map/ppermute | solution.py:19
  210.0 5.3 %collective-permute-start.15 = (f32[1,16,128,128]{3,2,1,0:T(8,128)S(1)}, f32[1,16,128,128]{3,2,1,0:T(8,128)S(1)}, u32[]{:S(2)}, u32[]{:S(2)}) collective-permute-start(f32[1,16,128,128]{3,2,1,0:T(8,128)S(1)} %get-tuple-element.23), channel_id=1, source_target_pairs={{0,1},{1,2},{2,3},{3,4},{4,5},{5,6},{6,7},{8,9},{9,10},{10,11},{11... | collective-permute-start | bytes 3145736 | tf_op jit(solution)/shard_map/ppermute | solution.py:16
  (6 other events, 13.3 us)
Sparse Core Ops, SparseCore 0:
  217.8 56.2 all-reduce.35
where the time goes:
time: 283 us; the launch traced here: 282 us
  blocking collectives  130 us (46%)
  waiting for transfers between devices  60.6 us (21%)
  starting transfers between devices  39.3 us (14%)
  other arithmetic  31.2 us (11%)
  between operations  14.7 us (5%)
  local copies, waits for them, and re-layouts  7.01 us (2%)
    psum x6, blocking collectives, pattern_sum(): return lax.psum(local_terms, 'vox')  117 us
    psum x1, waiting for transfers between devices, per_device(): gradient = lax.psum(local_gradient, 'pat')  56.4 us
    ppermute x8, starting transfers between devices, extended(): lax.ppermute(lax.slice_in_dim(block, block.shape[dim] - width, None, axis...  28.6 us
    psum x1, blocking collectives, per_device(): predicted = lax.psum(inner(probe_weights, forward), 'vox')  12.4 us
    ppermute x8, starting transfers between devices, extended(): lax.ppermute(lax.slice_in_dim(block, 0, width, axis=dim), axis, backward)  10.6 us
    reduce_sum x7, other arithmetic, inner(): return jnp.sum(left_factor * right_factor, axis=(0, 2, 3))  8.68 us
  transfers between devices with their start and end apart: 17, of which 5 were waited for; matrix products, arithmetic and copies ran while one was open for 6% of the time, Pallas kernels for 0%

commit v1 on v0

--- a/solution.py
+++ b/solution.py
@@ -6,6 +6,15 @@
 
 ITERS = 2
 leakage = 0.05
+
+
+def _begin_cycles(view):
+    v1 = view
+    n_parts = lax.axis_size("pat")
+    for j0 in [[(j, j ^ m) for j in range(n_parts)] for m in (1, 2, 4, 8, 16) if m < n_parts]:
+        wide_out = lax.ppermute(v1, axis_name="pat", perm=j0)
+        v1 = v1 + wide_out
+    return v1
 
 
 def extended(block, sides, width):
@@ -149,7 +158,7 @@
     local_gradient = -0.5 * (
         grad_depth + both_sides(row_products, 1) + both_sides(column_products, 2)
     )
-    gradient = lax.psum(local_gradient, "pat")
+    gradient = _begin_cycles(local_gradient)
     return (gradient, predicted)
 
 

time: 283 us -> 244 us (0.86)
  the two profiles are of different devices: /device:TPU:0 before, /device:TPU:4 now
where the time goes in v1:
time: 244 us; the launch traced here: 243 us
  blocking collectives  89.3 us (37%)
  waiting for transfers between devices  72.6 us (30%)
  starting transfers between devices  43.5 us (18%)
  other arithmetic  31.2 us (13%)
  local copies, waits for them, and re-layouts  5.44 us (2%)
    psum x6, blocking collectives, pattern_sum(): return lax.psum(local_terms, 'vox')  77.5 us
    ppermute x8, waiting for transfers between devices, extended(): lax.ppermute(lax.slice_in_dim(block, 0, width, axis=dim), axis, backward)  47.7 us
    ppermute x8, starting transfers between devices, extended(): lax.ppermute(lax.slice_in_dim(block, 0, width, axis=dim), axis, backward)  21.1 us
    ppermute x8, starting transfers between devices, extended(): lax.ppermute(lax.slice_in_dim(block, block.shape[dim] - width, None, axis...  17.6 us
    ppermute x8, waiting for transfers between devices, extended(): lax.ppermute(lax.slice_in_dim(block, block.shape[dim] - width, None, axis...  17.1 us
    psum x1, blocking collectives, per_device(): predicted = lax.psum(inner(probe_weights, forward), 'vox')  11.8 us
    reduce_sum x7, other arithmetic, inner(): return jnp.sum(left_factor * right_factor, axis=(0, 2, 3))  8.68 us
    ppermute x2, waiting for transfers between devices, _begin_cycles(): wide_out = lax.ppermute(v1, axis_name='pat', perm=j0)  7.74 us
  transfers between devices with their start and end apart: 18, of which 14 were waited for; matrix products, arithmetic and copies ran while one was open for 7% of the time, Pallas kernels for 0%

profile of v1, /device:TPU:4, one launch (start us, length us, event | category | flops | bytes accessed | tf_op | source)
XLA Modules:
  0.0 243.4 jit_solution(13638856616867834874)
XLA Ops:
  1.6 2.8 %collective-permute-start = (f32[1,128,128]{2,1,0:T(8,128)S(1)}, f32[1,128,128]{2,1,0:T(8,128)S(1)}, u32[]{:S(2)}, u32[]{:S(2)}) collective-permute-start(f32[1,128,128]{2,1,0:T(8,128)S(1)} %get-tuple-element.43), channel_id=1, source_target_pairs={{1,0},{2,1},{3,2},{4,3},{5,4},{6,5},{7,6},{9,8},{10,9},{11,10},{12... | collective-permute-start | bytes 196616 | tf_op jit(solution)/shard_map/ppermute | solution.py:28
  6.3 2.1 fusion.61
  8.4 4.7 %collective-permute-start.2 = (f32[1,8,128,128]{3,2,1,0:T(8,128)}, f32[1,8,128,128]{3,2,1,0:T(8,128)}, u32[]{:S(2)}, u32[]{:S(2)}) collective-permute-start(f32[1,8,128,128]{3,2,1,0:T(8,128)} %get-tuple-element.33), channel_id=1, source_target_pairs={{1,0},{2,1},{3,2},{4,3},{5,4},{6,5},{7,6},{9,8},{10,9},{11,10},{12... | collective-permute-start | bytes 1572872 | tf_op jit(solution)/shard_map/ppermute | solution.py:28
  20.0 4.8 %collective-permute-done.2 = f32[1,8,128,128]{3,2,1,0:T(8,128)} collective-permute-done((f32[1,8,128,128]{3,2,1,0:T(8,128)}, f32[1,8,128,128]{3,2,1,0:T(8,128)}, u32[]{:S(2)}, u32[]{:S(2)}) %collective-permute-start.2) | collective-permute-done | bytes 524320 | tf_op jit(solution)/shard_map/ppermute | solution.py:28
  28.1 3.9 %collective-permute-start.4 = (f32[1,8,128,128]{3,2,1,0:T(8,128)S(1)}, f32[1,8,128,128]{3,2,1,0:T(8,128)S(1)}, u32[]{:S(2)}, u32[]{:S(2)}) collective-permute-start(f32[1,8,128,128]{3,2,1,0:T(8,128)S(1)} %get-tuple-element.31), channel_id=1, source_target_pairs={{1,0},{2,1},{3,2},{4,3},{5,4},{6,5},{7,6},{9,8},{10,9},{11,10},{12... | collective-permute-start | bytes 1572872 | tf_op jit(solution)/shard_map/ppermute | solution.py:28
  34.6 7.7 %collective-permute-done.4 = f32[1,8,128,128]{3,2,1,0:T(8,128)S(1)} collective-permute-done((f32[1,8,128,128]{3,2,1,0:T(8,128)S(1)}, f32[1,8,128,128]{3,2,1,0:T(8,128)S(1)}, u32[]{:S(2)}, u32[]{:S(2)}) %collective-permute-start.4) | collective-permute-done | bytes 524320 | tf_op jit(solution)/shard_map/ppermute | solution.py:28
  45.4 13.3 %all-reduce.33 = (f32[8]{0:T(128)S(1)}, f32[8]{0:T(128)S(1)}) all-reduce(f32[8]{0:T(128)S(1)} %get-tuple-element.5, f32[8]{0:T(128)S(1)} %get-tuple-element.4), channel_id=1, replica_groups=mesh['pat'=4,'vox'=8] {'vox'}, use_global_device_ids=true, to_apply=%region_2.3 | all-reduce | flops 16 | bytes 128 | tf_op jit(solution)/shard_map/psum | solution.py:70
  62.2 16.4 %psum.65 = f32[8]{0:T(128)S(1)} all-reduce(f32[8]{0:T(128)S(1)} %multiply_reduce_fusion.4), channel_id=1, replica_groups=mesh['pat'=4,'vox'=8] {'vox'}, use_global_device_ids=true, to_apply=%region_6.7 | all-reduce | flops 8 | bytes 64 | tf_op jit(solution)/shard_map/psum | solution.py:70
  82.5 2.5 %collective-permute-start.7 = (f32[1,8,128,128]{3,2,1,0:T(8,128)S(1)}, f32[1,8,128,128]{3,2,1,0:T(8,128)S(1)}, u32[]{:S(2)}, u32[]{:S(2)}) collective-permute-start(f32[1,8,128,128]{3,2,1,0:T(8,128)S(1)} %get-tuple-element.28), channel_id=1, source_target_pairs={{0,1},{1,2},{2,3},{3,4},{4,5},{5,6},{6,7},{8,9},{9,10},{10,11},{11... | collective-permute-start | bytes 1572872 | tf_op jit(solution)/shard_map/ppermute | solution.py:25
  88.0 5.0 %collective-permute-done.6 = f32[1,8,128,128]{3,2,1,0:T(8,128)S(1)} collective-permute-done((f32[1,8,128,128]{3,2,1,0:T(8,128)S(1)}, f32[1,8,128,128]{3,2,1,0:T(8,128)S(1)}, u32[]{:S(2)}, u32[]{:S(2)}) %collective-permute-start.6) | collective-permute-done | bytes 524320 | tf_op jit(solution)/shard_map/ppermute | solution.py:28
  92.9 2.1 collective-permute-done.7
  95.0 2.8 %fusion.4 = (f32[3,8,128,128]{3,2,1,0:T(8,128)S(1)}, f32[3,8,128,128]{3,2,1,0:T(8,128)}) fusion(f32[1,8,128,128]{3,2,1,0:T(8,128)S(1)} %collective-permute-done.6, f32[2,8,128,128]{3,2,1,0:T(8,128)S(1)} %multiply_add_fusion.3, f32[1,8,128,128]{3,2,1,0:T(8,128)S(1)} %collective-permute-done.7, f32[3,128,128]{2,1,0:T(8,128)S(1)} %fusion.45, ...), kind=kLoop, calls=%fused_computation.13 | loop fusion | flops 3145728 | bytes 7536640 | tf_op jit(solution)/shard_map/mul | solution.py:52
  98.5 12.5 %psum.66 = f32[8]{0:T(128)S(1)} all-reduce(f32[8]{0:T(128)S(1)} %fusion.35), channel_id=1, replica_groups=mesh['pat'=4,'vox'=8] {'vox'}, use_global_device_ids=true, to_apply=%region_8.9 | all-reduce | flops 8 | bytes 64 | tf_op jit(solution)/shard_map/psum | solution.py:70
  111.0 2.8 %multiply_reduce_fusion.3 = (f32[8]{0:T(128)S(1)}, f32[2,8,128,128]{3,2,1,0:T(8,128)}) fusion(s32[2,128,128]{2,1,0:T(8,128)} %iota_add_fusion, s32[8]{0:T(128)S(1)} %get-tuple-element.45, s32[8]{0:T(128)S(1)} %get-tuple-element.46, f32[2,8,128,128]{3,2,1,0:T(8,128)S(1)} %multiply_add_fusion.3, f32[8]{0:T(128)S(1)} %div.49, ...), kind=kLoop, calls=%fused_computation.84 | loop fusion | flops 3145720 | bytes 4456608 | tf_op jit(solution)/shard_map/reduce_sum | solution.py:62
  113.8 11.8 %psum.67 = f32[8]{0:T(128)S(1)} all-reduce(f32[8]{0:T(128)S(1)} %get-tuple-element.15), channel_id=1, replica_groups=mesh['pat'=4,'vox'=8] {'vox'}, use_global_device_ids=true, to_apply=%region_10.11 | all-reduce | flops 8 | bytes 64 | tf_op jit(solution)/shard_map/psum | solution.py:135
  125.6 3.7 %broadcast_divide_fusion = (f32[2,8,128,128]{3,2,1,0:T(8,128)S(1)}, f32[2,8,128,128]{3,2,1,0:T(8,128)S(1)}) fusion(f32[2,128,128]{2,1,0:T(8,128)S(1)} %fusion.51, f32[2,8,128,127]{3,2,1,0:T(8,128)} %get-tuple-element.41, f32[2,8,127,128]{3,2,1,0:T(8,128)} %get-tuple-element.39, f32[3,8,128,128]{3,2,1,0:T(8,128)} %get-tuple-element.37, ...), kind=kLoop, calls=%fused_computation.94 | loop fusion | flops 3932160 | bytes 7585888 | tf_op jit(solution)/shard_map/div | solution.py:76
  131.4 2.5 %collective-permute-start.11 = (f32[1,8,128,128]{3,2,1,0:T(8,128)S(1)}, f32[1,8,128,128]{3,2,1,0:T(8,128)S(1)}, u32[]{:S(2)}, u32[]{:S(2)}) collective-permute-start(f32[1,8,128,128]{3,2,1,0:T(8,128)S(1)} %get-tuple-element.26), channel_id=1, source_target_pairs={{0,1},{1,2},{2,3},{3,4},{4,5},{5,6},{6,7},{8,9},{9,10},{10,11},{11... | collective-permute-start | bytes 1572872 | tf_op jit(solution)/shard_map/ppermute | solution.py:25
  134.5 6.2 %collective-permute-done.10 = f32[1,8,128,128]{3,2,1,0:T(8,128)S(1)} collective-permute-done((f32[1,8,128,128]{3,2,1,0:T(8,128)S(1)}, f32[1,8,128,128]{3,2,1,0:T(8,128)S(1)}, u32[]{:S(2)}, u32[]{:S(2)}) %collective-permute-start.10) | collective-permute-done | bytes 524320 | tf_op jit(solution)/shard_map/ppermute | solution.py:28
  140.7 4.4 %collective-permute-done.11 = f32[1,8,128,128]{3,2,1,0:T(8,128)S(1)} collective-permute-done((f32[1,8,128,128]{3,2,1,0:T(8,128)S(1)}, f32[1,8,128,128]{3,2,1,0:T(8,128)S(1)}, u32[]{:S(2)}, u32[]{:S(2)}) %collective-permute-start.11) | collective-permute-done | bytes 524320 | tf_op jit(solution)/shard_map/ppermute | solution.py:25
  146.1 11.8 %all-reduce.32 = (f32[8]{0:T(128)S(1)}, f32[8]{0:T(128)S(1)}) all-reduce(f32[8]{0:T(128)S(1)} %get-tuple-element.3, f32[8]{0:T(128)S(1)} %get-tuple-element.2), channel_id=1, replica_groups=mesh['pat'=4,'vox'=8] {'vox'}, use_global_device_ids=true, to_apply=%region_12.13 | all-reduce | flops 16 | bytes 128 | tf_op jit(solution)/shard_map/psum | solution.py:70
  158.3 11.8 %psum.70 = f32[8]{0:T(128)S(1)} all-reduce(f32[8]{0:T(128)S(1)} %multiply_reduce_fusion), channel_id=1, replica_groups=mesh['pat'=4,'vox'=8] {'vox'}, use_global_device_ids=true, to_apply=%region_16.17 | all-reduce | flops 8 | bytes 64 | tf_op jit(solution)/shard_map/psum | solution.py:70
  171.7 2.1 collective-permute-start.12
  173.8 2.4 collective-permute-start.13
  176.7 6.6 %collective-permute-done.12 = f32[1,8,128,128]{3,2,1,0:T(8,128)S(1)} collective-permute-done((f32[1,8,128,128]{3,2,1,0:T(8,128)S(1)}, f32[1,8,128,128]{3,2,1,0:T(8,128)S(1)}, u32[]{:S(2)}, u32[]{:S(2)}) %collective-permute-start.12) | collective-permute-done | bytes 524320 | tf_op jit(solution)/shard_map/ppermute | solution.py:28
  183.3 3.5 %collective-permute-done.13 = f32[1,8,128,128]{3,2,1,0:T(8,128)S(1)} collective-permute-done((f32[1,8,128,128]{3,2,1,0:T(8,128)S(1)}, f32[1,8,128,128]{3,2,1,0:T(8,128)S(1)}, u32[]{:S(2)}, u32[]{:S(2)}) %collective-permute-start.13) | collective-permute-done | bytes 524320 | tf_op jit(solution)/shard_map/ppermute | solution.py:25
  187.7 11.8 %psum.71 = f32[8]{0:T(128)S(1)} all-reduce(f32[8]{0:T(128)S(1)} %fusion.19), channel_id=1, replica_groups=mesh['pat'=4,'vox'=8] {'vox'}, use_global_device_ids=true, to_apply=%region_18.19 | all-reduce | flops 8 | bytes 64 | tf_op jit(solution)/shard_map/psum | solution.py:70
  202.9 2.4 collective-permute-start.15
  206.2 17.4 %collective-permute-done.14 = f32[1,16,128,128]{3,2,1,0:T(8,128)S(1)} collective-permute-done((f32[1,16,128,128]{3,2,1,0:T(8,128)S(1)}, f32[1,16,128,128]{3,2,1,0:T(8,128)S(1)}, u32[]{:S(2)}, u32[]{:S(2)}) %collective-permute-start.14) | collective-permute-done | bytes 1048608 | tf_op jit(solution)/shard_map/ppermute | solution.py:28
  223.6 4.9 %collective-permute-done.15 = f32[1,16,128,128]{3,2,1,0:T(8,128)S(1)} collective-permute-done((f32[1,16,128,128]{3,2,1,0:T(8,128)S(1)}, f32[1,16,128,128]{3,2,1,0:T(8,128)S(1)}, u32[]{:S(2)}, u32[]{:S(2)}) %collective-permute-start.15) | collective-permute-done | bytes 1048608 | tf_op jit(solution)/shard_map/ppermute | solution.py:25
  231.8 3.4 %collective-permute-done.16 = f32[2,128,128]{2,1,0:T(8,128)S(1)} collective-permute-done((f32[2,128,128]{2,1,0:T(8,128)S(1)}, f32[2,128,128]{2,1,0:T(8,128)S(1)}, u32[]{:S(2)}, u32[]{:S(2)}) %collective-permute-start.16) | collective-permute-done | bytes 131104 | tf_op jit(solution)/shard_map/ppermute | solution.py:15
  235.2 3.2 %collective-permute-start.17 = (f32[2,128,128]{2,1,0:T(8,128)S(1)}, f32[2,128,128]{2,1,0:T(8,128)S(1)}, u32[]{:S(2)}, u32[]{:S(2)}) collective-permute-start(f32[2,128,128]{2,1,0:T(8,128)S(1)} %add.274), channel_id=1, source_target_pairs={{0,16},{8,24},{16,0},{24,8},{1,17},{9,25},{17,1},{25,9},{2,18},{10... | collective-permute-start | bytes 393224 | tf_op jit(solution)/shard_map/ppermute | solution.py:15
  238.4 4.4 %collective-permute-done.17 = f32[2,128,128]{2,1,0:T(8,128)S(1)} collective-permute-done((f32[2,128,128]{2,1,0:T(8,128)S(1)}, f32[2,128,128]{2,1,0:T(8,128)S(1)}, u32[]{:S(2)}, u32[]{:S(2)}) %collective-permute-start.17) | collective-permute-done | bytes 131104 | tf_op jit(solution)/shard_map/ppermute | solution.py:15
  (114 shorter events, 44.7 us)
Async XLA Ops:
  0.6 14.4 %copy-start = (f32[2,8,128,128]{3,2,1,0:T(8,128)S(1)}, f32[2,8,128,128]{3,2,1,0:T(8,128)}, u32[]{:S(2)}) copy-start(f32[2,8,128,128]{3,2,1,0:T(8,128)} %param.8) | copy-start | bytes 3145732
  1.6 18.2 %collective-permute-start = (f32[1,128,128]{2,1,0:T(8,128)S(1)}, f32[1,128,128]{2,1,0:T(8,128)S(1)}, u32[]{:S(2)}, u32[]{:S(2)}) collective-permute-start(f32[1,128,128]{2,1,0:T(8,128)S(1)} %get-tuple-element.43), channel_id=1, source_target_pairs={{1,0},{2,1},{3,2},{4,3},{5,4},{6,5},{7,6},{9,8},{10,9},{11,10},{12... | collective-permute-start | bytes 196616 | tf_op jit(solution)/shard_map/ppermute | solution.py:28
  4.4 15.4 %collective-permute-start.1 = (f32[1,128,128]{2,1,0:T(8,128)S(1)}, f32[1,128,128]{2,1,0:T(8,128)S(1)}, u32[]{:S(2)}, u32[]{:S(2)}) collective-permute-start(f32[1,128,128]{2,1,0:T(8,128)S(1)} %get-tuple-element.42), channel_id=1, source_target_pairs={{0,1},{1,2},{2,3},{3,4},{4,5},{5,6},{6,7},{8,9},{9,10},{10,11},{11... | collective-permute-start | bytes 196616 | tf_op jit(solution)/shard_map/ppermute | solution.py:25
  8.4 9.6 %copy-start.15 = (f32[2,128,128]{2,1,0:T(8,128)S(1)}, f32[2,128,128]{2,1,0:T(8,128)}, u32[]{:S(2)}) copy-start(f32[2,128,128]{2,1,0:T(8,128)} %param.6) | copy-start | bytes 393220
  8.4 10.5 %copy-start.17 = (s32[8,4]{0,1:T(4,128)S(1)}, s32[8,4]{0,1:T(4,128)}, u32[]{:S(2)}) copy-start(s32[8,4]{0,1:T(4,128)} %param.10) | copy-start | bytes 388
  8.4 10.5 %copy-start.18 = (s32[128]{0:T(128)S(1)}, s32[128]{0:T(128)}, u32[]{:S(2)}) copy-start(s32[128]{0:T(128)} %param.9) | copy-start | bytes 1540
  8.4 10.8 %copy-start.1 = (f32[2,8,128,128]{3,2,1,0:T(8,128)S(1)}, f32[2,8,128,128]{3,2,1,0:T(8,128)}, u32[]{:S(2)}) copy-start(f32[2,8,128,128]{3,2,1,0:T(8,128)} %param.7) | copy-start | bytes 3145732
  8.4 16.4 %collective-permute-start.2 = (f32[1,8,128,128]{3,2,1,0:T(8,128)}, f32[1,8,128,128]{3,2,1,0:T(8,128)}, u32[]{:S(2)}, u32[]{:S(2)}) collective-permute-start(f32[1,8,128,128]{3,2,1,0:T(8,128)} %get-tuple-element.33), channel_id=1, source_target_pairs={{1,0},{2,1},{3,2},{4,3},{5,4},{6,5},{7,6},{9,8},{10,9},{11,10},{12... | collective-permute-start | bytes 1572872 | tf_op jit(solution)/shard_map/ppermute | solution.py:28
  13.1 12.7 %collective-permute-start.3 = (f32[1,8,128,128]{3,2,1,0:T(8,128)S(1)}, f32[1,8,128,128]{3,2,1,0:T(8,128)}, u32[]{:S(2)}, u32[]{:S(2)}) collective-permute-start(f32[1,8,128,128]{3,2,1,0:T(8,128)S(1)} %get-tuple-element.32), channel_id=1, source_target_pairs={{0,1},{1,2},{2,3},{3,4},{4,5},{5,6},{6,7},{8,9},{9,10},{10,11},{11... | collective-permute-start | bytes 1572872 | tf_op jit(solution)/shard_map/ppermute | solution.py:25
  16.1 71.8 %collective-permute-start.9 = (f32[1,8,128,128]{3,2,1,0:T(8,128)}, f32[1,8,128,128]{3,2,1,0:T(8,128)}, u32[]{:S(2)}, u32[]{:S(2)}) collective-permute-start(f32[1,8,128,128]{3,2,1,0:T(8,128)} %get-tuple-element.34), channel_id=1, source_target_pairs={{0,1},{1,2},{2,3},{3,4},{4,5},{5,6},{6,7},{8,9},{9,10},{10,11},{11... | collective-permute-start | bytes 1572872 | tf_op jit(solution)/shard_map/ppermute | solution.py:25
  20.0 7.2 %copy-start.16 = (s32[2,128,128]{2,1,0:T(8,128)S(1)}, s32[2,128,128]{2,1,0:T(8,128)}, u32[]{:S(2)}) copy-start(s32[2,128,128]{2,1,0:T(8,128)} %iota_add_fusion) | copy-start | bytes 393220
  28.0 30.7 %copy-start.3 = (f32[2,8,128,128]{3,2,1,0:T(8,128)}, f32[2,8,128,128]{3,2,1,0:T(8,128)S(1)}, u32[]{:S(2)}) copy-start(f32[2,8,128,128]{3,2,1,0:T(8,128)S(1)} %get-tuple-element.19) | copy-start | bytes 3145732
  28.0 6.0 %copy-start.11 = (f32[2,128,127]{2,1,0:T(8,128)S(1)}, f32[2,128,127]{2,1,0:T(8,128)}, u32[]{:S(2)}) copy-start(f32[2,128,127]{2,1,0:T(8,128)} %copy-done.10) | copy-start | bytes 390148
  28.1 14.1 %collective-permute-start.4 = (f32[1,8,128,128]{3,2,1,0:T(8,128)S(1)}, f32[1,8,128,128]{3,2,1,0:T(8,128)S(1)}, u32[]{:S(2)}, u32[]{:S(2)}) collective-permute-start(f32[1,8,128,128]{3,2,1,0:T(8,128)S(1)} %get-tuple-element.31), channel_id=1, source_target_pairs={{1,0},{2,1},{3,2},{4,3},{5,4},{6,5},{7,6},{9,8},{10,9},{11,10},{12... | collective-permute-start | bytes 1572872 | tf_op jit(solution)/shard_map/ppermute | solution.py:28
  32.0 11.5 %collective-permute-start.5 = (f32[1,8,128,128]{3,2,1,0:T(8,128)S(1)}, f32[1,8,128,128]{3,2,1,0:T(8,128)S(1)}, u32[]{:S(2)}, u32[]{:S(2)}) collective-permute-start(f32[1,8,128,128]{3,2,1,0:T(8,128)S(1)} %get-tuple-element.30), channel_id=1, source_target_pairs={{0,1},{1,2},{2,3},{3,4},{4,5},{5,6},{6,7},{8,9},{9,10},{10,11},{11... | collective-permute-start | bytes 1572872 | tf_op jit(solution)/shard_map/ppermute | solution.py:25
  60.3 27.6 %collective-permute-start.8 = (f32[1,8,128,128]{3,2,1,0:T(8,128)}, f32[1,8,128,128]{3,2,1,0:T(8,128)}, u32[]{:S(2)}, u32[]{:S(2)}) collective-permute-start(f32[1,8,128,128]{3,2,1,0:T(8,128)} %get-tuple-element.35), channel_id=1, source_target_pairs={{1,0},{2,1},{3,2},{4,3},{5,4},{6,5},{7,6},{9,8},{10,9},{11,10},{12... | collective-permute-start | bytes 1572872 | tf_op jit(solution)/shard_map/ppermute | solution.py:28
  80.5 4.6 %copy-start.12 = (f32[2,128,127]{2,1,0:T(8,128)S(1)}, f32[2,128,127]{2,1,0:T(8,128)}, u32[]{:S(2)}) copy-start(f32[2,128,127]{2,1,0:T(8,128)} %copy-done.10) | copy-start | bytes 390148
  80.6 12.3 %collective-permute-start.6 = (f32[1,8,128,128]{3,2,1,0:T(8,128)S(1)}, f32[1,8,128,128]{3,2,1,0:T(8,128)S(1)}, u32[]{:S(2)}, u32[]{:S(2)}) collective-permute-start(f32[1,8,128,128]{3,2,1,0:T(8,128)S(1)} %get-tuple-element.29), channel_id=1, source_target_pairs={{1,0},{2,1},{3,2},{4,3},{5,4},{6,5},{7,6},{9,8},{10,9},{11,10},{12... | collective-permute-start | bytes 1572872 | tf_op jit(solution)/shard_map/ppermute | solution.py:28
  82.5 4.2 %copy-start.7 = (f32[2,127,128]{2,1,0:T(8,128)S(1)}, f32[2,127,128]{2,1,0:T(8,128)}, u32[]{:S(2)}) copy-start(f32[2,127,128]{2,1,0:T(8,128)} %copy-done.5) | copy-start | bytes 390148
  82.5 12.5 %collective-permute-start.7 = (f32[1,8,128,128]{3,2,1,0:T(8,128)S(1)}, f32[1,8,128,128]{3,2,1,0:T(8,128)S(1)}, u32[]{:S(2)}, u32[]{:S(2)}) collective-permute-start(f32[1,8,128,128]{3,2,1,0:T(8,128)S(1)} %get-tuple-element.28), channel_id=1, source_target_pairs={{0,1},{1,2},{2,3},{3,4},{4,5},{5,6},{6,7},{8,9},{9,10},{10,11},{11... | collective-permute-start | bytes 1572872 | tf_op jit(solution)/shard_map/ppermute | solution.py:25
  111.0 14.6 %copy-start.19 = (f32[8]{0:T(128)S(1)}, f32[8]{0:T(128)}, u32[]{:S(2)}) copy-start(f32[8]{0:T(128)} %param.11) | copy-start | bytes 100
  129.4 4.6 %copy-start.13 = (f32[2,128,127]{2,1,0:T(8,128)S(1)}, f32[2,128,127]{2,1,0:T(8,128)}, u32[]{:S(2)}) copy-start(f32[2,128,127]{2,1,0:T(8,128)} %copy-done.10) | copy-start | bytes 390148
  129.5 11.3 %collective-permute-start.10 = (f32[1,8,128,128]{3,2,1,0:T(8,128)S(1)}, f32[1,8,128,128]{3,2,1,0:T(8,128)S(1)}, u32[]{:S(2)}, u32[]{:S(2)}) collective-permute-start(f32[1,8,128,128]{3,2,1,0:T(8,128)S(1)} %get-tuple-element.27), channel_id=1, source_target_pairs={{1,0},{2,1},{3,2},{4,3},{5,4},{6,5},{7,6},{9,8},{10,9},{11,10},{12... | collective-permute-start | bytes 1572872 | tf_op jit(solution)/shard_map/ppermute | solution.py:28
  131.4 13.7 %collective-permute-start.11 = (f32[1,8,128,128]{3,2,1,0:T(8,128)S(1)}, f32[1,8,128,128]{3,2,1,0:T(8,128)S(1)}, u32[]{:S(2)}, u32[]{:S(2)}) collective-permute-start(f32[1,8,128,128]{3,2,1,0:T(8,128)S(1)} %get-tuple-element.26), channel_id=1, source_target_pairs={{0,1},{1,2},{2,3},{3,4},{4,5},{5,6},{6,7},{8,9},{9,10},{10,11},{11... | collective-permute-start | bytes 1572872 | tf_op jit(solution)/shard_map/ppermute | solution.py:25
  146.1 24.0 %copy-start.4 = (f32[2,8,128,128]{3,2,1,0:T(8,128)}, f32[2,8,128,128]{3,2,1,0:T(8,128)S(1)}, u32[]{:S(2)}) copy-start(f32[2,8,128,128]{3,2,1,0:T(8,128)S(1)} %get-tuple-element.12) | copy-start | bytes 3145732
  171.6 4.6 %copy-start.14 = (f32[2,128,127]{2,1,0:T(8,128)S(1)}, f32[2,128,127]{2,1,0:T(8,128)}, u32[]{:S(2)}) copy-start(f32[2,128,127]{2,1,0:T(8,128)} %copy-done.10) | copy-start | bytes 390148
  171.7 11.6 %collective-permute-start.12 = (f32[1,8,128,128]{3,2,1,0:T(8,128)S(1)}, f32[1,8,128,128]{3,2,1,0:T(8,128)S(1)}, u32[]{:S(2)}, u32[]{:S(2)}) collective-permute-start(f32[1,8,128,128]{3,2,1,0:T(8,128)S(1)} %get-tuple-element.25), channel_id=1, source_target_pairs={{1,0},{2,1},{3,2},{4,3},{5,4},{6,5},{7,6},{9,8},{10,9},{11,10},{12... | collective-permute-start | bytes 1572872 | tf_op jit(solution)/shard_map/ppermute | solution.py:28
  173.8 13.0 %collective-permute-start.13 = (f32[1,8,128,128]{3,2,1,0:T(8,128)S(1)}, f32[1,8,128,128]{3,2,1,0:T(8,128)S(1)}, u32[]{:S(2)}, u32[]{:S(2)}) collective-permute-start(f32[1,8,128,128]{3,2,1,0:T(8,128)S(1)} %get-tuple-element.24), channel_id=1, source_target_pairs={{0,1},{1,2},{2,3},{3,4},{4,5},{5,6},{6,7},{8,9},{9,10},{10,11},{11... | collective-permute-start | bytes 1572872 | tf_op jit(solution)/shard_map/ppermute | solution.py:25
  200.9 22.6 %collective-permute-start.14 = (f32[1,16,128,128]{3,2,1,0:T(8,128)S(1)}, f32[1,16,128,128]{3,2,1,0:T(8,128)S(1)}, u32[]{:S(2)}, u32[]{:S(2)}) collective-permute-start(f32[1,16,128,128]{3,2,1,0:T(8,128)S(1)} %get-tuple-element.22), channel_id=1, source_target_pairs={{1,0},{2,1},{3,2},{4,3},{5,4},{6,5},{7,6},{9,8},{10,9},{11,10},{12... | collective-permute-start | bytes 3145736 | tf_op jit(solution)/shard_map/ppermute | solution.py:28
  202.9 25.6 %collective-permute-start.15 = (f32[1,16,128,128]{3,2,1,0:T(8,128)S(1)}, f32[1,16,128,128]{3,2,1,0:T(8,128)S(1)}, u32[]{:S(2)}, u32[]{:S(2)}) collective-permute-start(f32[1,16,128,128]{3,2,1,0:T(8,128)S(1)} %get-tuple-element.23), channel_id=1, source_target_pairs={{0,1},{1,2},{2,3},{3,4},{4,5},{5,6},{6,7},{8,9},{9,10},{10,11},{11... | collective-permute-start | bytes 3145736 | tf_op jit(solution)/shard_map/ppermute | solution.py:25
  230.1 5.0 %collective-permute-start.16 = (f32[2,128,128]{2,1,0:T(8,128)S(1)}, f32[2,128,128]{2,1,0:T(8,128)S(1)}, u32[]{:S(2)}, u32[]{:S(2)}) collective-permute-start(f32[2,128,128]{2,1,0:T(8,128)S(1)} %fusion.48), channel_id=1, source_target_pairs={{0,8},{8,0},{16,24},{24,16},{1,9},{9,1},{17,25},{25,17},{2,10},{10... | collective-permute-start | bytes 393224 | tf_op jit(solution)/shard_map/ppermute | solution.py:15
  235.2 7.5 %collective-permute-start.17 = (f32[2,128,128]{2,1,0:T(8,128)S(1)}, f32[2,128,128]{2,1,0:T(8,128)S(1)}, u32[]{:S(2)}, u32[]{:S(2)}) collective-permute-start(f32[2,128,128]{2,1,0:T(8,128)S(1)} %add.274), channel_id=1, source_target_pairs={{0,16},{8,24},{16,0},{24,8},{1,17},{9,25},{17,1},{25,9},{2,18},{10... | collective-permute-start | bytes 393224 | tf_op jit(solution)/shard_map/ppermute | solution.py:15
  (7 other events, 16.6 us)
